TPU v7x, 256 devices: a whole 4x4x8 slice. The times are simulated.
256 devices in a mesh: row: 16 (over x, z_lo, core), col: 16 (over y, z_hi).
Axes of the slice: x: 4, y: 4, z: 8 (z_hi: 4, z_lo: 2; z = z_hi * 2 + z_lo), core: 2. Of those that a mesh axis runs over, the one named last changes fastest.
Arguments:
- ancestor_inverse: bfloat16 [32768, 32768], P('row', 'col'), may hold values from -0.03125 to 0.03125
- panel: bfloat16 [32768, 512], P(('row', 'col')), may hold values from -0.75 to 0.75
- structure: int32 [2, 128], replicated, may hold values 0 or 1
- diag_inverse: float32 [2, 256, 256], replicated, may hold values from -6 to 6
Outputs:
- upper: bfloat16 [32768, 512], P(('row', 'col'))
- diagonal: float32 [2, 256, 256], replicated
All inputs are finite; a program needn't handle non-finite values.
Results may differ from a plain program's by a relative error of at most 0.0014.
Values may be sent and summed in bfloat16 or wider, within the bound.
A program may use at most 64 MiB of HBM per device.

v0:
```python
import jax
import jax.numpy as jnp
from jax import lax
from jax.sharding import PartitionSpec as P


def row_keep(begin_row, length, structure, blk_width):
    blocks_all = structure.shape[1]
    indices = begin_row + jnp.arange(length, dtype=jnp.int32)
    owners = indices // blk_width
    onehot = (owners[:, None] == jnp.arange(blocks_all, dtype=jnp.int32)[None, :]).astype(
        jnp.float32
    )
    keeps = jnp.dot(onehot, structure.T.astype(jnp.float32), preferred_element_type=jnp.float32)
    return jnp.repeat(keeps, blk_width, axis=1)


def diag_part(lower, upper_rows, blk_width):
    snodes = upper_rows.shape[1] // blk_width
    lower_f = lower.astype(jnp.float32).reshape(lower.shape[0], snodes, blk_width)
    upper_f = upper_rows.reshape(upper_rows.shape[0], snodes, blk_width)
    return jnp.einsum("mkw,mkv->kwv", lower_f, upper_f, precision=lax.Precision.HIGHEST)


def local(ancestor_inverse, panel, structure, diag_inverse):
    blk_width = diag_inverse.shape[1]
    row_count = lax.axis_size("row")
    col_count = lax.axis_size("col")
    row_index = lax.axis_index("row")
    col_index = lax.axis_index("col")
    piece_rows = panel.shape[0]
    begin_own = (row_index * col_count + col_index) * piece_rows
    keep_own = row_keep(begin_own, piece_rows, structure, blk_width)
    masked = panel * keep_own.astype(jnp.bfloat16)
    flip = [
        (r * col_count + c, c * row_count + r) for r in range(row_count) for c in range(col_count)
    ]
    moved = lax.ppermute(masked, ("row", "col"), flip)
    col_block = lax.all_gather(moved, "row", axis=0, tiled=True)
    partial_rows = -jnp.dot(ancestor_inverse, col_block, preferred_element_type=jnp.float32)
    own_rows = lax.psum_scatter(partial_rows, "col", scatter_dimension=0, tiled=True)
    diag_sum = lax.psum(diag_part(masked, own_rows, blk_width), ("row", "col"))
    upper = (own_rows * keep_own).astype(jnp.bfloat16)
    diagonal = diag_inverse - diag_sum
    return (upper, diagonal)


def solution(mesh):
    return jax.shard_map(
        local,
        mesh=mesh,
        in_specs=(P("row", "col"), P(("row", "col"), None), P(), P()),
        out_specs=(P(("row", "col"), None), P()),
        check_vma=False,
    )
```

profile of v0, /device:TPU:2, one launch (start us, length us, event | category | flops | bytes accessed | tf_op | source)
XLA Modules:
  0.0 442.1 jit_solution(1587222471581334880)
XLA Ops:
  7.2 0.0 all-gather.2.cloned.1.call-start
  7.2 1.0 copy.6
  8.3 0.9 fusion.2
  9.2 3.5 collective-permute-start
  12.6 4.3 collective-permute-done
  17.0 0.0 copy-start.1
  17.0 0.7 copy-done.1
  17.6 0.0 all-gather.2.cloned.1.call-update
  17.6 0.0 reduce-scatter.2.cloned.1.call-start
  17.7 48.5 %all-gather.2.cloned.1.call-done = bf16[2048,512]{0,1:T(8,128)(2,1)} async-done(((bf16[128,512]{0,1:T(8,128)(2,1)}), bf16[2048,512]{0,1:T(8,128)(2,1)}) %all-gather.2.cloned.1.call-update) | async-done | bytes 2097168 | tf_op jit(solution)/shard_map/all_gather | solution.py:39
  66.2 10.5 %negate_bitcast_fusion = f32[2048,512]{0,1:T(8,128)} fusion(bf16[2048,512]{0,1:T(8,128)(2,1)} %all-gather.2.cloned.1.call-done, bf16[2048,2048]{1,0:T(8,128)(2,1)} %param.4), kind=kOutput, calls=%fused_computation | convolution fusion | flops 4296015872 | bytes 14680064 | tf_op jit(solution)/shard_map/dot_general | solution.py:40
  76.7 0.0 copy-start
  76.7 0.0 reduce-scatter.2.cloned.1.call-update
  76.7 0.0 all-reduce.2.cloned.1.call-start
  76.8 97.6 %reduce-scatter.2.cloned.1.call-done = f32[128,512]{0,1:T(8,128)} async-done(((f32[2048,512]{0,1:T(8,128)}), f32[128,512]{0,1:T(8,128)}) %reduce-scatter.2.cloned.1.call-update) | async-done | bytes 262160 | tf_op jit(solution)/shard_map/reduce_scatter | solution.py:41
  174.4 2.1 fusion.5
  176.5 0.0 all-reduce.2.cloned.1.call-update
  176.6 1.0 fusion
  177.5 0.8 copy.8
  178.3 255.4 %all-reduce.2.cloned.1.call-done = f32[2,256,256]{2,1,0:T(8,128)} async-done(((f32[2,256,256]{2,1,0:T(8,128)}), f32[2,256,256]{2,1,0:T(8,128)}) %all-reduce.2.cloned.1.call-update) | async-done | bytes 524304 | tf_op jit(solution)/shard_map/psum | solution.py:42
  433.7 0.0 copy-done
  433.7 1.9 sub.10
  (2 shorter events, 0.0 us)
Async XLA Ops:
  7.2 59.0 %all-gather.2.cloned.1.call-start = ((), (), s32[]{:S(2)}) async-start(), calls=%async_computation.1 | async-start | bytes 2228224 | tf_op jit(solution)/shard_map/all_gather | solution.py:39
  9.2 7.8 %collective-permute-start = (bf16[128,512]{0,1:T(8,128)(2,1)S(1)}, bf16[128,512]{0,1:T(8,128)(2,1)S(1)}, u32[]{:S(2)}, u32[]{:S(2)}) collective-permute-start(bf16[128,512]{0,1:T(8,128)(2,1)S(1)} %fusion.1), channel_id=1, source_target_pairs={{0,0},{1,16},{2,32},{3,48},{4,64},{5,80},{6,96},{7,112},{8,128},{9... | collective-permute-start | bytes 393224 | tf_op jit(solution)/shard_map/ppermute | solution.py:38
  17.0 0.7 copy-start.1
  17.6 156.8 %reduce-scatter.2.cloned.1.call-start = ((), (), s32[]{:S(2)}) async-start(), calls=%async_computation.2 | async-start | bytes 4456448 | tf_op jit(solution)/shard_map/reduce_scatter | solution.py:41
  76.7 357.0 %copy-start = (f32[2,256,256]{2,1,0:T(8,128)S(1)}, f32[2,256,256]{2,1,0:T(8,128)}, u32[]{:S(2)}) copy-start(f32[2,256,256]{2,1,0:T(8,128)} %param.7) | copy-start | bytes 1572868
  76.7 356.9 %all-reduce.2.cloned.1.call-start = ((), (), s32[]{:S(2)}) async-start(), calls=%async_computation.3 | async-start | bytes 1048576 | tf_op jit(solution)/shard_map/psum | solution.py:42
Sparse Core Ops, SparseCore 0:
  17.8 48.4 all-gather.1
  76.8 97.5 reduce-scatter.1
  180.4 253.1 all-reduce.1
where the time goes:
time: 442 us
  waiting for transfers between devices  406 us (92%)
  between operations  13.8 us (3%)
  matrix products  13.5 us (3%)
    psum x1, waiting for transfers between devices, local(): diag_sum = lax.psum(diag_part(masked, own_rows, blk_width), ('row', 'col'))  255 us
    reduce_scatter x1, waiting for transfers between devices, local(): lax.psum_scatter(partial_rows, 'col', scatter_dimension=0, tiled=True)  97.6 us
    all_gather x1, waiting for transfers between devices, local(): col_block = lax.all_gather(moved, 'row', axis=0, tiled=True)  48.5 us
    dot_general x1, matrix products, local(): jnp.dot(ancestor_inverse, col_block, preferred_element_type=jnp.float32)  10.5 us
  transfers between devices with their start and end apart: 4, of which 4 were waited for; matrix products, arithmetic and copies ran while one was open for 0% of the time, Pallas kernels for 0%

commit v1 on v0

--- a/solution.py
+++ b/solution.py
@@ -2,6 +2,7 @@
 import jax.numpy as jnp
 from jax import lax
 from jax.sharding import PartitionSpec as P
+from jax.lax import psum
 
 
 def row_keep(begin_row, length, structure, blk_width):
@@ -39,7 +40,8 @@
     col_block = lax.all_gather(moved, "row", axis=0, tiled=True)
     partial_rows = -jnp.dot(ancestor_inverse, col_block, preferred_element_type=jnp.float32)
     own_rows = lax.psum_scatter(partial_rows, "col", scatter_dimension=0, tiled=True)
-    diag_sum = lax.psum(diag_part(masked, own_rows, blk_width), ("row", "col"))
+    frame = diag_part(masked, own_rows, blk_width)
+    diag_sum = psum(psum(frame, "col"), "row")
     upper = (own_rows * keep_own).astype(jnp.bfloat16)
     diagonal = diag_inverse - diag_sum
     return (upper, diagonal)

time: 442 us -> 476 us (1.077); the launches traced: 442 us -> 470 us
  waiting for transfers between devices: 406 us -> 434 us
    psum x1 -> x2, waiting for transfers between devices: 255 us -> 283 us  [local(): diag_sum = psum(psum(frame, 'col'), 'row')]
  transfers between devices with their start and end apart: 4 -> 5, of which waited for: 4 -> 5; matrix products, arithmetic and copies ran while one was open for 0% -> 0% of each run, Pallas kernels for 0% -> 0%
where the time goes in v1:
time: 476 us; the launch traced here: 470 us
  waiting for transfers between devices  434 us (91%)
  between operations  13.8 us (3%)
  matrix products  13.5 us (3%)
    psum x2, waiting for transfers between devices, local(): diag_sum = psum(psum(frame, 'col'), 'row')  283 us
    reduce_scatter x1, waiting for transfers between devices, local(): lax.psum_scatter(partial_rows, 'col', scatter_dimension=0, tiled=True)  97.6 us
    all_gather x1, waiting for transfers between devices, local(): col_block = lax.all_gather(moved, 'row', axis=0, tiled=True)  48.5 us
    dot_general x1, matrix products, local(): jnp.dot(ancestor_inverse, col_block, preferred_element_type=jnp.float32)  10.5 us
  transfers between devices with their start and end apart: 5, of which 5 were waited for; matrix products, arithmetic and copies ran while one was open for 0% of the time, Pallas kernels for 0%

profile of v1, /device:TPU:2, one launch (start us, length us, event | category | flops | bytes accessed | tf_op | source)
XLA Modules:
  0.0 470.0 jit_solution(18138829594782750900)
XLA Ops:
  7.2 0.0 all-gather.2.cloned.1.call-start
  7.2 1.0 copy.6
  8.3 0.9 fusion.2
  9.2 3.5 collective-permute-start
  12.6 4.3 collective-permute-done
  17.0 0.0 copy-start.1
  17.0 0.7 copy-done.1
  17.6 0.0 all-gather.2.cloned.1.call-update
  17.6 0.0 reduce-scatter.2.cloned.1.call-start
  17.7 48.5 %all-gather.2.cloned.1.call-done = bf16[2048,512]{0,1:T(8,128)(2,1)} async-done(((bf16[128,512]{0,1:T(8,128)(2,1)}), bf16[2048,512]{0,1:T(8,128)(2,1)}) %all-gather.2.cloned.1.call-update) | async-done | bytes 2097168 | tf_op jit(solution)/shard_map/all_gather | solution.py:40
  66.2 10.5 %negate_bitcast_fusion = f32[2048,512]{0,1:T(8,128)} fusion(bf16[2048,512]{0,1:T(8,128)(2,1)} %all-gather.2.cloned.1.call-done, bf16[2048,2048]{1,0:T(8,128)(2,1)} %param.4), kind=kOutput, calls=%fused_computation | convolution fusion | flops 4296015872 | bytes 14680064 | tf_op jit(solution)/shard_map/dot_general | solution.py:41
  76.7 0.0 copy-start
  76.7 0.0 reduce-scatter.2.cloned.1.call-update
  76.7 0.0 all-reduce.3.cloned.1.call-start
  76.8 97.6 %reduce-scatter.2.cloned.1.call-done = f32[128,512]{0,1:T(8,128)} async-done(((f32[2048,512]{0,1:T(8,128)}), f32[128,512]{0,1:T(8,128)}) %reduce-scatter.2.cloned.1.call-update) | async-done | bytes 262160 | tf_op jit(solution)/shard_map/reduce_scatter | solution.py:42
  174.4 2.1 fusion.5
  176.5 0.0 all-reduce.3.cloned.1.call-update
  176.6 0.0 all-reduce.5.cloned.1.call-start
  176.6 167.2 %all-reduce.3.cloned.1.call-done = f32[2,256,256]{2,1,0:T(8,128)} async-done(((f32[2,256,256]{2,1,0:T(8,128)}), f32[2,256,256]{2,1,0:T(8,128)}) %all-reduce.3.cloned.1.call-update) | async-done | bytes 524304 | tf_op jit(solution)/shard_map/psum | solution.py:44
  343.8 0.0 all-reduce.5.cloned.1.call-update
  343.9 1.0 fusion
  344.8 0.8 copy.8
  345.6 116.0 %all-reduce.5.cloned.1.call-done = f32[2,256,256]{2,1,0:T(8,128)} async-done(((f32[2,256,256]{2,1,0:T(8,128)}), f32[2,256,256]{2,1,0:T(8,128)}) %all-reduce.5.cloned.1.call-update) | async-done | bytes 524304 | tf_op jit(solution)/shard_map/psum | solution.py:44
  461.6 0.0 copy-done
  461.6 1.9 sub.10
  (2 shorter events, 0.0 us)
Async XLA Ops:
  7.2 59.0 %all-gather.2.cloned.1.call-start = ((), (), s32[]{:S(2)}) async-start(), calls=%async_computation.1 | async-start | bytes 2228224 | tf_op jit(solution)/shard_map/all_gather | solution.py:40
  9.2 7.8 %collective-permute-start = (bf16[128,512]{0,1:T(8,128)(2,1)S(1)}, bf16[128,512]{0,1:T(8,128)(2,1)S(1)}, u32[]{:S(2)}, u32[]{:S(2)}) collective-permute-start(bf16[128,512]{0,1:T(8,128)(2,1)S(1)} %fusion.1), channel_id=1, source_target_pairs={{0,0},{1,16},{2,32},{3,48},{4,64},{5,80},{6,96},{7,112},{8,128},{9... | collective-permute-start | bytes 393224 | tf_op jit(solution)/shard_map/ppermute | solution.py:39
  17.0 0.7 copy-start.1
  17.6 156.8 %reduce-scatter.2.cloned.1.call-start = ((), (), s32[]{:S(2)}) async-start(), calls=%async_computation.2 | async-start | bytes 4456448 | tf_op jit(solution)/shard_map/reduce_scatter | solution.py:42
  76.7 384.9 %copy-start = (f32[2,256,256]{2,1,0:T(8,128)S(1)}, f32[2,256,256]{2,1,0:T(8,128)}, u32[]{:S(2)}) copy-start(f32[2,256,256]{2,1,0:T(8,128)} %param.7) | copy-start | bytes 1572868
  76.7 267.1 %all-reduce.3.cloned.1.call-start = ((), (), s32[]{:S(2)}) async-start(), calls=%async_computation.3 | async-start | bytes 1048576 | tf_op jit(solution)/shard_map/psum | solution.py:44
  176.6 285.0 %all-reduce.5.cloned.1.call-start = ((), (), s32[]{:S(2)}) async-start(), calls=%async_computation.4 | async-start | bytes 1048576 | tf_op jit(solution)/shard_map/psum | solution.py:44
Sparse Core Ops, SparseCore 0:
  17.8 48.4 all-gather.1
  76.8 97.5 reduce-scatter.1
  177.6 166.1 all-reduce.2
  346.3 115.2 all-reduce.4

commit v2 on v0

--- a/solution.py
+++ b/solution.py
@@ -36,7 +36,9 @@
         (r * col_count + c, c * row_count + r) for r in range(row_count) for c in range(col_count)
     ]
     moved = lax.ppermute(masked, ("row", "col"), flip)
-    col_block = lax.all_gather(moved, "row", axis=0, tiled=True)
+    q_next = jnp.stack([moved for _ in range(lax.psum(1, axis_name="row"))])
+    outcome_arr = lax.all_to_all(q_next, axis_name="row", split_axis=0, concat_axis=0)
+    col_block = jnp.concatenate(outcome_arr, axis=0)
     partial_rows = -jnp.dot(ancestor_inverse, col_block, preferred_element_type=jnp.float32)
     own_rows = lax.psum_scatter(partial_rows, "col", scatter_dimension=0, tiled=True)
     diag_sum = lax.psum(diag_part(masked, own_rows, blk_width), ("row", "col"))

time: 442 us -> 432 us (0.977)
  waiting for transfers between devices: 406 us -> 355 us
  blocking collectives: 0 us -> 41.5 us
    all_gather x1 -> x0, waiting for transfers between devices: 48.5 us -> none  [local(): col_block = lax.all_gather(moved, 'row', axis=0, tiled=True)]
    all_to_all x0 -> x1, blocking collectives: none -> 41.5 us  [local(): lax.all_to_all(q_next, axis_name='row', split_axis=0, concat_axis=0)]
  transfers between devices with their start and end apart: 4 -> 3, of which waited for: 4 -> 3; matrix products, arithmetic and copies ran while one was open for 0% -> 0% of each run, Pallas kernels for 0% -> 0%
where the time goes in v2:
time: 432 us; the launch traced here: 431 us
  waiting for transfers between devices  355 us (82%)
  blocking collectives  41.5 us (10%)
  between operations  14.1 us (3%)
  matrix products  12.6 us (3%)
    psum x1, waiting for transfers between devices, local(): diag_sum = lax.psum(diag_part(masked, own_rows, blk_width), ('row', 'col'))  255 us
    reduce_scatter x1, waiting for transfers between devices, local(): lax.psum_scatter(partial_rows, 'col', scatter_dimension=0, tiled=True)  94.9 us
    all_to_all x1, blocking collectives, local(): lax.all_to_all(q_next, axis_name='row', split_axis=0, concat_axis=0)  41.5 us
    dot_general x1, matrix products, local(): jnp.dot(ancestor_inverse, col_block, preferred_element_type=jnp.float32)  9.61 us
  transfers between devices with their start and end apart: 3, of which 3 were waited for; matrix products, arithmetic and copies ran while one was open for 0% of the time, Pallas kernels for 0%

profile of v2, /device:TPU:2, one launch (start us, length us, event | category | flops | bytes accessed | tf_op | source)
XLA Modules:
  0.0 431.3 jit_solution(409576046637895446)
XLA Ops:
  7.2 0.0 reduce-scatter.2.cloned.1.call-start
  7.2 1.0 copy.6
  8.3 0.9 fusion.2
  9.2 3.5 collective-permute-start
  12.6 4.3 collective-permute-done
  17.0 0.1 copy.7
  17.1 0.2 stack.2
  17.3 41.5 %all_to_all.5 = bf16[16,128,512]{2,1,0:T(8,128)(2,1)S(1)} all-to-all(bf16[16,128,512]{2,1,0:T(8,128)(2,1)S(1)} %stack.2), channel_id=1, replica_groups=mesh['row'=16,'col'=16] {'row'}, dimensions={0} | all-to-all | bytes 4194304 | tf_op jit(solution)/shard_map/all_to_all | solution.py:40
  58.8 9.6 %negate_bitcast_fusion = f32[2048,512]{0,1:T(8,128)} fusion(bf16[2048,512]{1,0:T(8,128)(2,1)S(1)} %bitcast.16, bf16[2048,2048]{1,0:T(8,128)(2,1)} %param.4), kind=kOutput, calls=%fused_computation | convolution fusion | flops 4296015872 | bytes 14680064 | tf_op jit(solution)/shard_map/dot_general | solution.py:42
  68.4 0.0 copy-start
  68.4 0.0 reduce-scatter.2.cloned.1.call-update
  68.4 0.0 all-reduce.2.cloned.1.call-start
  68.5 94.9 %reduce-scatter.2.cloned.1.call-done = f32[128,512]{0,1:T(8,128)} async-done(((f32[2048,512]{0,1:T(8,128)}), f32[128,512]{0,1:T(8,128)}) %reduce-scatter.2.cloned.1.call-update) | async-done | bytes 262160 | tf_op jit(solution)/shard_map/reduce_scatter | solution.py:43
  163.4 2.1 fusion.5
  165.5 0.0 all-reduce.2.cloned.1.call-update
  165.5 1.0 fusion
  166.5 0.8 copy.9
  167.3 255.3 %all-reduce.2.cloned.1.call-done = f32[2,256,256]{2,1,0:T(8,128)} async-done(((f32[2,256,256]{2,1,0:T(8,128)}), f32[2,256,256]{2,1,0:T(8,128)}) %all-reduce.2.cloned.1.call-update) | async-done | bytes 524304 | tf_op jit(solution)/shard_map/psum | solution.py:44
  422.6 0.0 copy-done
  422.6 1.9 sub.10
  (2 shorter events, 0.0 us)
Async XLA Ops:
  7.2 156.2 %reduce-scatter.2.cloned.1.call-start = ((), (), s32[]{:S(2)}) async-start(), calls=%async_computation.2 | async-start | bytes 4456448 | tf_op jit(solution)/shard_map/reduce_scatter | solution.py:43
  9.2 7.8 %collective-permute-start = (bf16[128,512]{0,1:T(8,128)(2,1)S(1)}, bf16[128,512]{0,1:T(8,128)(2,1)S(1)}, u32[]{:S(2)}, u32[]{:S(2)}) collective-permute-start(bf16[128,512]{0,1:T(8,128)(2,1)S(1)} %fusion.1), channel_id=1, source_target_pairs={{0,0},{1,16},{2,32},{3,48},{4,64},{5,80},{6,96},{7,112},{8,128},{9... | collective-permute-start | bytes 393224 | tf_op jit(solution)/shard_map/ppermute | solution.py:38
  68.4 354.2 %copy-start = (f32[2,256,256]{2,1,0:T(8,128)S(1)}, f32[2,256,256]{2,1,0:T(8,128)}, u32[]{:S(2)}) copy-start(f32[2,256,256]{2,1,0:T(8,128)} %param.7) | copy-start | bytes 1572868
  68.4 354.2 %all-reduce.2.cloned.1.call-start = ((), (), s32[]{:S(2)}) async-start(), calls=%async_computation.3 | async-start | bytes 1048576 | tf_op jit(solution)/shard_map/psum | solution.py:44
Sparse Core Ops, SparseCore 0:
  68.5 94.7 reduce-scatter.1
  169.4 253.1 all-reduce.1
